TPU v7x, 32 devices: a whole 2x2x4 slice. The times are simulated.
32 devices in a mesh: tm: 16 (over z, y, core), strip: 2 (over x).
Axes of the slice: x: 2, y: 2, z: 4, core: 2. Of those that a mesh axis runs over, the one named last changes fastest.
Arguments:
- forward_u: float32 [16, 128, 1024], P('tm', 'strip'), may hold values from -4 to 4
- forward_v: float32 [16, 128, 1024], P('tm', 'strip'), may hold values from -4 to 4
- permittivity: float32 [128, 1024], P('strip'), may hold values from 1 to 3
- coarse_rate: float32 [16, 128, 1024], P('tm', 'strip'), may hold values from 0.2 to 8
- modulation: float32 [32], replicated, may hold values from 0 to 0.3
- tile_map: int32 [1, 8], replicated, may hold values from 0 to 31
- start_step: int32 [16], P('tm'), may hold values from 0 to 255
Outputs:
- adjoint_u: float32 [16, 128, 1024], P('tm', 'strip')
- adjoint_v: float32 [16, 128, 1024], P('tm', 'strip')
- depth_grad: float32 [32], replicated
Inputs may be any that keep to these rules, and one draw needn't show every extreme that they name: `tile_map`: tile parameter indices. `start_step`: start steps within one period.
All inputs are finite; a program needn't handle non-finite values.
Results may differ from a plain program's by a relative error of at most 0.0003.
Values sent between devices are 32-bit elements; how exact they have to be, the bound alone decides.
A program may use at most 128 MiB of HBM per device.

v0:
```python
import jax
import jax.numpy as jnp
from jax import lax
from jax.sharding import PartitionSpec as P

TILE = 128
STEPS = 2
STENCIL = 4
PERIOD = 256


stencil_coef = (-205.0 / 72.0, 8.0 / 5.0, -1.0 / 5.0, 8.0 / 315.0, -1.0 / 560.0)
time_step = 0.4
damping_rate = 0.1


def padded_2(cells, sides, width):
    for axis, dim in sides:
        count = lax.axis_size(axis)
        ends = count - 1
        head = lax.slice_in_dim(cells, 0, width, axis=dim)
        tail = lax.slice_in_dim(cells, cells.shape[dim] - width, cells.shape[dim], axis=dim)
        cells = jnp.concatenate(
            [
                lax.ppermute(tail, axis, [(i, (i + 1) % count) for i in range(ends)]),
                cells,
                lax.ppermute(head, axis, [((i + 1) % count, i) for i in range(ends)]),
            ],
            axis=dim,
        )
    return cells


def from_behind(array, axis, by):
    length = lax.axis_size(axis)
    return lax.ppermute(array, axis, [(i, (i + by) % length) for i in range(length)])


def entering(part, axis, combine, identity, reverse):
    count = lax.axis_size(axis)
    place = lax.axis_index(axis)
    ahead = count - 1 - place if reverse else place
    gathered = jax.tree.map(lambda a: lax.all_gather(a, axis), part)
    state = jax.tree.map(lambda a, e: jnp.zeros_like(a) + jnp.asarray(e, a.dtype), part, identity)

    def one(turn, state):
        source = count - 1 - turn if reverse else turn
        return combine(
            state, jax.tree.map(lambda a: lax.dynamic_index_in_dim(a, source, 0, False), gathered)
        )

    return lax.fori_loop(0, ahead, one, state)


def laplacian_rows(padded, rim_width):
    row_count = padded.shape[0] - 2 * rim_width
    center = padded[rim_width : rim_width + row_count]
    summed = 2.0 * stencil_coef[0] * center
    for offset in range(1, 5):
        along_x = (
            padded[rim_width + offset : rim_width + offset + row_count]
            + padded[rim_width - offset : rim_width - offset + row_count]
        )
        along_y = jnp.roll(center, offset, axis=1) + jnp.roll(center, -offset, axis=1)
        summed = summed + stencil_coef[offset] * (along_x + along_y)
    return summed


def row_selector(first_row, row_count, tile_rows):
    global_rows = first_row + jnp.arange(row_count, dtype=jnp.int32)
    tile_index = global_rows // TILE
    return (tile_index[:, None] == jnp.arange(tile_rows, dtype=jnp.int32)[None, :]).astype(
        jnp.float32
    )


def rows_depth(first_row, row_count, tile_depth):
    selector = row_selector(first_row, row_count, tile_depth.shape[0])
    per_tile = jnp.dot(selector, tile_depth, precision=lax.Precision.HIGHEST)
    return jnp.repeat(per_tile, TILE, axis=1)


def compose_high(earlier, latter):
    return (latter[0] * earlier[0], latter[0][None] * earlier[1] + latter[1])


def compose_low(earlier, latter):
    return (earlier[0] * latter[0], earlier[0][None] * latter[1] + earlier[1])


def shards(forward_u, forward_v, permittivity, coarse_rate, modulation, tile_map, start_step):
    start_u = forward_u[0]
    start_v = forward_v[0]
    strip_rows = start_u.shape[0]
    strip_place = lax.axis_index("strip")
    slice_count = lax.axis_size("tm")
    selector_params = (
        tile_map[:, :, None] == jnp.arange(modulation.shape[0], dtype=jnp.int32)[None, None, :]
    ).astype(jnp.float32)
    tile_depth = jnp.sum(selector_params * modulation[None, None, :], axis=2)
    cell_depth = rows_depth(strip_place * strip_rows, strip_rows, tile_depth)
    offsets = (start_step[0] + jnp.arange(STEPS, dtype=jnp.int32)).astype(jnp.float32)
    cosines = jnp.cos(2.0 * jnp.pi / PERIOD * offsets)
    eps_list = [permittivity * (1.0 + cell_depth * cosines[level]) for level in range(STEPS)]
    forcings = []
    field_u = start_u
    field_v = start_v
    for level in range(STEPS):
        padded = padded_2(field_u, (("strip", 0),), STENCIL)
        forcing = laplacian_rows(padded, STENCIL) - damping_rate * field_v
        forcings.append(forcing)
        field_v = field_v + time_step * forcing / eps_list[level]
        field_u = field_u + time_step * field_v
    following = from_behind(jnp.stack([start_u, start_v]), "tm", -1)
    mismatch = jnp.stack([field_u, field_v]) - following
    retain = jnp.exp(-coarse_rate[0] / slice_count)
    ones = jnp.ones_like(retain)
    zeros = jnp.zeros_like(mismatch)
    higher_a, higher_b = entering((retain, mismatch), "tm", compose_high, (ones, zeros), True)
    lower_a, lower_b = entering((retain, mismatch), "tm", compose_low, (ones, zeros), False)
    cycle_a = retain * higher_a * lower_a
    cycle_b = retain[None] * (higher_a[None] * lower_b + higher_b) + mismatch
    coarse = cycle_b / (1.0 - cycle_a)[None]
    preceding = from_behind(coarse, "tm", 1)
    gradient_cells = jnp.zeros_like(start_u)
    back_u = coarse[0]
    back_v = coarse[1]
    for level in reversed(range(STEPS)):
        eps_now = eps_list[level]
        total_v = back_v + time_step * back_u
        weighted = time_step / eps_now * total_v
        padded = padded_2(weighted, (("strip", 0),), STENCIL)
        back_u = back_u + laplacian_rows(padded, STENCIL)
        back_v = (1.0 - time_step * damping_rate / eps_now) * total_v
        gradient_cells = gradient_cells - cosines[level] * time_step * total_v * forcings[level] / (
            eps_now * eps_now
        )
    cell_terms = gradient_cells * permittivity
    column_sums = jnp.sum(cell_terms.reshape(strip_rows, cell_terms.shape[1] // TILE, TILE), axis=2)
    selector = row_selector(strip_place * strip_rows, strip_rows, tile_map.shape[0])
    tile_part = jnp.dot(selector.T, column_sums, precision=lax.Precision.HIGHEST)
    param_part = jnp.sum(selector_params * tile_part[:, :, None], axis=(0, 1))
    depth_grad = lax.psum(param_part, ("tm", "strip"))
    adjoint_u = back_u - preceding[0]
    adjoint_v = back_v - preceding[1]
    return (adjoint_u[None], adjoint_v[None], depth_grad)


def solution(mesh):
    placed = (
        P("tm", "strip", None),
        P("tm", "strip", None),
        P("strip", None),
        P("tm", "strip", None),
        P(),
        P(),
        P("tm"),
    )
    return jax.shard_map(
        shards,
        mesh=mesh,
        in_specs=placed,
        out_specs=(P("tm", "strip", None), P("tm", "strip", None), P()),
        check_vma=False,
    )
```

profile of v0, /device:TPU:0, one launch (start us, length us, event | category | flops | bytes accessed | tf_op | source)
XLA Modules:
  0.0 250.6 jit_solution(9343302233114372609)
XLA Ops:
  7.2 1.8 fusion.108
  9.9 4.9 %collective-permute-start.1 = (f32[4,1024]{1,0:T(4,128)S(1)}, f32[4,1024]{1,0:T(4,128)S(1)}, u32[]{:S(2)}, u32[]{:S(2)}) collective-permute-start(f32[4,1024]{1,0:T(4,128)S(1)} %get-tuple-element.229), channel_id=1, source_target_pairs={{0,1},{2,3},{4,5},{6,7},{8,9},{10,11},{12,13},{14,15},{16,17},{18,... | collective-permute-start | bytes 49160 | tf_op jit(solution)/shard_map/ppermute | solution.py:25
  14.7 1.3 collective-permute-start
  16.0 1.9 pad_maximum_fusion
  17.9 3.7 %collective-permute-start.4 = (f32[2,64,1024]{2,1,0:T(8,128)}, f32[2,64,1024]{2,1,0:T(8,128)S(1)}, u32[]{:S(2)}, u32[]{:S(2)}) collective-permute-start(f32[2,64,1024]{2,1,0:T(8,128)} %pad_maximum_fusion), channel_id=1, source_target_pairs={{0,30},{2,0},{4,2},{6,4},{8,6},{10,8},{12,10},{14,12},{16,14},{18,... | collective-permute-start | bytes 1572872 | tf_op jit(solution)/shard_map/ppermute | solution.py:36
  31.9 1.3 fusion.99
  33.5 4.0 %multiply_add_fusion.1 = (f32[64,1024]{1,0:T(8,128)S(1)}, f32[64,1024]{1,0:T(8,128)S(1)}, f32[64,1024]{1,0:T(8,128)}, f32[64,1024]{1,0:T(8,128)S(1)}) fusion(f32[1,64,1024]{2,1,0:T(8,128)} %param.11, f32[1,64,1024]{2,1,0:T(8,128)} %param.12, f32[64,4]{1,0:T(8,128)S(1)} %get-tuple-element.231, f32[64,1020]{1,0:T(8,128)S(1)} %get-tuple-element.233, ...), kind=kLoop, calls=%fused_computation.193 | loop fusion | flops 2949120 | bytes 4489216 | tf_op jit(solution)/shard_map/add | solution.py:113
  37.5 4.3 %collective-permute-start.3 = (f32[4,1024]{1,0:T(4,128)S(1)}, f32[4,1024]{1,0:T(4,128)S(1)}, u32[]{:S(2)}, u32[]{:S(2)}) collective-permute-start(f32[4,1024]{1,0:T(4,128)S(1)} %get-tuple-element.211), channel_id=1, source_target_pairs={{0,1},{2,3},{4,5},{6,7},{8,9},{10,11},{12,13},{14,15},{16,17},{18,... | collective-permute-start | bytes 49160 | tf_op jit(solution)/shard_map/ppermute | solution.py:25
  41.8 1.3 collective-permute-start.2
  43.9 3.5 %collective-permute-done.2 = f32[4,1024]{1,0:T(4,128)S(1)} collective-permute-done((f32[4,1024]{1,0:T(4,128)S(1)}, f32[4,1024]{1,0:T(4,128)S(1)}, u32[]{:S(2)}, u32[]{:S(2)}) %collective-permute-start.2) | collective-permute-done | bytes 16416 | tf_op jit(solution)/shard_map/ppermute | solution.py:27
  50.4 15.8 %all-gather.4.cloned.1.call-done = f32[16,64,1024]{2,1,0:T(8,128)} async-done(((f32[1,64,1024]{2,1,0:T(8,128)}), f32[16,64,1024]{2,1,0:T(8,128)}) %all-gather.4.cloned.1.call-update) | async-done | bytes 4194320 | tf_op jit(solution)/shard_map/all_gather | solution.py:43
  66.2 75.0 %all-gather.6.cloned.1.call-done = f32[32,64,1024]{2,1,0:T(8,128)} async-done(((f32[2,64,1024]{2,1,0:T(8,128)}), f32[32,64,1024]{2,1,0:T(8,128)}) %all-gather.6.cloned.1.call-update) | async-done | bytes 8388624 | tf_op jit(solution)/shard_map/all_gather | solution.py:43
  141.3 35.1 %while.26 = (s32[]{:T(128)}, f32[64,1024]{1,0:T(8,128)S(1)}, f32[2,64,1024]{2,1,0:T(8,128)S(1)}, s32[]{:T(128)}, f32[16,64,1024]{2,1,0:T(8,128)}, /*index=5*/f32...) while((s32[]{:T(128)}, f32[64,1024]{1,0:T(8,128)S(1)}, f32[2,64,1024]{2,1,0:T(8,128)S(1)}, ...), condition=%wide.region_2.3_spmd, body=%wide.region_1.2_spmd.sunk | while | flops 327686 | bytes 2883747 | solution.py:52
  144.7 1.3 bitcast_add_fusion.4
  177.4 1.4 add_divide_fusion
  179.7 3.4 %collective-permute-start.6 = (f32[4,1024]{1,0:T(4,128)S(1)}, f32[4,1024]{1,0:T(4,128)S(1)}, u32[]{:S(2)}, u32[]{:S(2)}) collective-permute-start(f32[4,1024]{1,0:T(4,128)S(1)} %get-tuple-element.191), channel_id=1, source_target_pairs={{0,1},{2,3},{4,5},{6,7},{8,9},{10,11},{12,13},{14,15},{16,17},{18,... | collective-permute-start | bytes 49160 | tf_op jit(solution)/shard_map/ppermute | solution.py:25
  183.0 1.3 collective-permute-start.5
  184.5 4.2 %collective-permute-done.5 = f32[4,1024]{1,0:T(4,128)S(1)} collective-permute-done((f32[4,1024]{1,0:T(4,128)S(1)}, f32[4,1024]{1,0:T(4,128)S(1)}, u32[]{:S(2)}, u32[]{:S(2)}) %collective-permute-start.5) | collective-permute-done | bytes 16416 | tf_op jit(solution)/shard_map/ppermute | solution.py:27
  189.8 39.4 %psum.7 = f32[32]{0:T(128)} all-reduce(f32[32]{0:T(128)S(1)} %select_reduce_fusion), channel_id=1, replica_groups=mesh['tm'=16,'strip'=2] {'tm','strip'}, use_global_device_ids=true, to_apply=%region_7.8 | all-reduce | flops 32 | bytes 256 | tf_op jit(solution)/shard_map/psum | solution.py:143
  229.2 1.7 fusion.84
  231.7 4.2 %collective-permute-start.8 = (f32[4,1024]{1,0:T(4,128)S(1)}, f32[4,1024]{1,0:T(4,128)S(1)}, u32[]{:S(2)}, u32[]{:S(2)}) collective-permute-start(f32[4,1024]{1,0:T(4,128)S(1)} %get-tuple-element.177), channel_id=1, source_target_pairs={{0,1},{2,3},{4,5},{6,7},{8,9},{10,11},{12,13},{14,15},{16,17},{18,... | collective-permute-start | bytes 49160 | tf_op jit(solution)/shard_map/ppermute | solution.py:25
  235.9 1.3 collective-permute-start.7
  237.3 4.2 %collective-permute-done.7 = f32[4,1024]{1,0:T(4,128)S(1)} collective-permute-done((f32[4,1024]{1,0:T(4,128)S(1)}, f32[4,1024]{1,0:T(4,128)S(1)}, u32[]{:S(2)}, u32[]{:S(2)}) %collective-permute-start.7) | collective-permute-done | bytes 16416 | tf_op jit(solution)/shard_map/ppermute | solution.py:27
  241.5 2.2 fusion.9
  (110 shorter events, 50.7 us)
Async XLA Ops:
  7.2 59.0 %all-gather.4.cloned.1.call-start = ((), (), s32[]{:S(2)}) async-start(), calls=%async_computation | async-start | bytes 4456448 | tf_op jit(solution)/shard_map/all_gather | solution.py:43
  9.0 38.5 %copy-start = (f32[64,1024]{1,0:T(8,128)S(1)}, f32[64,1024]{1,0:T(8,128)}, u32[]{:S(2)}) copy-start(f32[64,1024]{1,0:T(8,128)} %param.13) | copy-start | bytes 786436
  9.0 132.2 %all-gather.6.cloned.1.call-start = ((), (), s32[]{:S(2)}) async-start(), calls=%async_computation.1 | async-start | bytes 8912896 | tf_op jit(solution)/shard_map/all_gather | solution.py:43
  9.9 23.5 %collective-permute-start.1 = (f32[4,1024]{1,0:T(4,128)S(1)}, f32[4,1024]{1,0:T(4,128)S(1)}, u32[]{:S(2)}, u32[]{:S(2)}) collective-permute-start(f32[4,1024]{1,0:T(4,128)S(1)} %get-tuple-element.229), channel_id=1, source_target_pairs={{0,1},{2,3},{4,5},{6,7},{8,9},{10,11},{12,13},{14,15},{16,17},{18,... | collective-permute-start | bytes 49160 | tf_op jit(solution)/shard_map/ppermute | solution.py:25
  14.7 18.6 %collective-permute-start = (f32[4,1024]{1,0:T(4,128)S(1)}, f32[4,1024]{1,0:T(4,128)S(1)}, u32[]{:S(2)}, u32[]{:S(2)}) collective-permute-start(f32[4,1024]{1,0:T(4,128)S(1)} %get-tuple-element.228), channel_id=1, source_target_pairs={{1,0},{3,2},{5,4},{7,6},{9,8},{11,10},{13,12},{15,14},{17,16},{19,... | collective-permute-start | bytes 49160 | tf_op jit(solution)/shard_map/ppermute | solution.py:27
  17.9 30.3 %collective-permute-start.4 = (f32[2,64,1024]{2,1,0:T(8,128)}, f32[2,64,1024]{2,1,0:T(8,128)S(1)}, u32[]{:S(2)}, u32[]{:S(2)}) collective-permute-start(f32[2,64,1024]{2,1,0:T(8,128)} %pad_maximum_fusion), channel_id=1, source_target_pairs={{0,30},{2,0},{4,2},{6,4},{8,6},{10,8},{12,10},{14,12},{16,14},{18,... | collective-permute-start | bytes 1572872 | tf_op jit(solution)/shard_map/ppermute | solution.py:36
  37.5 6.4 %collective-permute-start.3 = (f32[4,1024]{1,0:T(4,128)S(1)}, f32[4,1024]{1,0:T(4,128)S(1)}, u32[]{:S(2)}, u32[]{:S(2)}) collective-permute-start(f32[4,1024]{1,0:T(4,128)S(1)} %get-tuple-element.211), channel_id=1, source_target_pairs={{0,1},{2,3},{4,5},{6,7},{8,9},{10,11},{12,13},{14,15},{16,17},{18,... | collective-permute-start | bytes 49160 | tf_op jit(solution)/shard_map/ppermute | solution.py:25
  41.8 5.6 %collective-permute-start.2 = (f32[4,1024]{1,0:T(4,128)S(1)}, f32[4,1024]{1,0:T(4,128)S(1)}, u32[]{:S(2)}, u32[]{:S(2)}) collective-permute-start(f32[4,1024]{1,0:T(4,128)S(1)} %get-tuple-element.210), channel_id=1, source_target_pairs={{1,0},{3,2},{5,4},{7,6},{9,8},{11,10},{13,12},{15,14},{17,16},{19,... | collective-permute-start | bytes 49160 | tf_op jit(solution)/shard_map/ppermute | solution.py:27
  48.2 93.0 %copy-start.1 = (f32[2,64,1024]{2,1,0:T(8,128)}, f32[2,64,1024]{2,1,0:T(8,128)S(1)}, u32[]{:S(2)}) copy-start(f32[2,64,1024]{2,1,0:T(8,128)S(1)} %collective-permute-done.4) | copy-start | bytes 1572868
  176.4 1.0 copy-start.3
  176.5 12.2 %copy-start.2 = (f32[64,1024]{1,0:T(8,128)S(1)}, f32[64,1024]{1,0:T(8,128)}, u32[]{:S(2)}) copy-start(f32[64,1024]{1,0:T(8,128)} %get-tuple-element.156) | copy-start | bytes 786436
  176.5 13.2 %copy-start.4 = (s32[1,8]{1,0:T(1,128)S(1)}, s32[1,8]{1,0:T(1,128)}, u32[]{:S(2)}) copy-start(s32[1,8]{1,0:T(1,128)} %param.16) | copy-start | bytes 100
  179.7 4.8 %collective-permute-start.6 = (f32[4,1024]{1,0:T(4,128)S(1)}, f32[4,1024]{1,0:T(4,128)S(1)}, u32[]{:S(2)}, u32[]{:S(2)}) collective-permute-start(f32[4,1024]{1,0:T(4,128)S(1)} %get-tuple-element.191), channel_id=1, source_target_pairs={{0,1},{2,3},{4,5},{6,7},{8,9},{10,11},{12,13},{14,15},{16,17},{18,... | collective-permute-start | bytes 49160 | tf_op jit(solution)/shard_map/ppermute | solution.py:25
  183.0 5.6 %collective-permute-start.5 = (f32[4,1024]{1,0:T(4,128)S(1)}, f32[4,1024]{1,0:T(4,128)S(1)}, u32[]{:S(2)}, u32[]{:S(2)}) collective-permute-start(f32[4,1024]{1,0:T(4,128)S(1)} %get-tuple-element.190), channel_id=1, source_target_pairs={{1,0},{3,2},{5,4},{7,6},{9,8},{11,10},{13,12},{15,14},{17,16},{19,... | collective-permute-start | bytes 49160 | tf_op jit(solution)/shard_map/ppermute | solution.py:27
  184.4 44.8 %collective-permute-start.9 = (f32[2,64,1024]{2,1,0:T(8,128)S(1)}, f32[2,64,1024]{2,1,0:T(8,128)}, u32[]{:S(2)}, u32[]{:S(2)}) collective-permute-start(f32[2,64,1024]{2,1,0:T(8,128)S(1)} %add_divide_fusion), channel_id=1, source_target_pairs={{0,2},{2,4},{4,6},{6,8},{8,10},{10,12},{12,14},{14,16},{16,18},{18... | collective-permute-start | bytes 1572872 | tf_op jit(solution)/shard_map/ppermute | solution.py:36
  231.7 5.6 %collective-permute-start.8 = (f32[4,1024]{1,0:T(4,128)S(1)}, f32[4,1024]{1,0:T(4,128)S(1)}, u32[]{:S(2)}, u32[]{:S(2)}) collective-permute-start(f32[4,1024]{1,0:T(4,128)S(1)} %get-tuple-element.177), channel_id=1, source_target_pairs={{0,1},{2,3},{4,5},{6,7},{8,9},{10,11},{12,13},{14,15},{16,17},{18,... | collective-permute-start | bytes 49160 | tf_op jit(solution)/shard_map/ppermute | solution.py:25
  235.9 5.6 %collective-permute-start.7 = (f32[4,1024]{1,0:T(4,128)S(1)}, f32[4,1024]{1,0:T(4,128)S(1)}, u32[]{:S(2)}, u32[]{:S(2)}) collective-permute-start(f32[4,1024]{1,0:T(4,128)S(1)} %get-tuple-element.176), channel_id=1, source_target_pairs={{1,0},{3,2},{5,4},{7,6},{9,8},{11,10},{13,12},{15,14},{17,16},{19,... | collective-permute-start | bytes 49160 | tf_op jit(solution)/shard_map/ppermute | solution.py:27
Sparse Core Ops, SparseCore 0:
  10.1 56.0 all-gather.3
  68.4 72.8 all-gather.5
where the time goes:
time: 253 us; the launch traced here: 251 us
  waiting for transfers between devices  103 us (41%)
  other arithmetic  52.5 us (21%)
  blocking collectives  39.4 us (16%)
  starting transfers between devices  25.6 us (10%)
  between operations  16.3 us (6%)
  local copies, waits for them, and re-layouts  13.4 us (5%)
    all_gather x2, waiting for transfers between devices, entering(): gathered = jax.tree.map(lambda a: lax.all_gather(a, axis), part)  90.8 us
    psum x1, blocking collectives, shards(): depth_grad = lax.psum(param_part, ('tm', 'strip'))  39.4 us
    add x15, other arithmetic, compose_high(): return (latter[0] * earlier[0], latter[0][None] * earlier[1] + latter[1])  19.3 us
    ppermute x4, starting transfers between devices, padded_2(): lax.ppermute(tail, axis, [(i, (i + 1) % count) for i in range(ends)])  16.7 us
    mul x15, other arithmetic, compose_high(): return (latter[0] * earlier[0], latter[0][None] * earlier[1] + latter[1])  15.4 us
    ppermute x4, waiting for transfers between devices, padded_2(): lax.ppermute(head, axis, [((i + 1) % count, i) for i in range(ends)])  11.9 us
    slice x24, local copies, waits for them, and re-layouts, laplacian_rows(): jnp.roll(center, offset, axis=1) + jnp.roll(center, -offset, axis=1)  9.75 us
    ppermute x4, starting transfers between devices, padded_2(): lax.ppermute(head, axis, [((i + 1) % count, i) for i in range(ends)])  5.17 us
  transfers between devices with their start and end apart: 12, of which 5 were waited for; matrix products, arithmetic and copies ran while one was open for 9% of the time, Pallas kernels for 0%

commit v1 on v0

v1 whole, which is shorter than its diff:
```python
import functools

import jax
import jax.numpy as jnp
from jax import lax
from jax.experimental import pallas as pl
from jax.experimental.pallas import tpu as pltpu
from jax.sharding import PartitionSpec as P

TILE = 128
STEPS = 2
STENCIL = 4
PERIOD = 256
RIM = STEPS * STENCIL
BASE = 2 * RIM

stencil_coef = (-205.0 / 72.0, 8.0 / 5.0, -1.0 / 5.0, 8.0 / 315.0, -1.0 / 560.0)
time_step = 0.4
damping_rate = 0.1

MESH = pl.DeviceIdType.MESH


def laplacian(ref, base):
    center = ref[base : base + 8, :]
    cols = center.shape[1]
    summed = (2.0 * stencil_coef[0]) * center
    for o in range(1, STENCIL + 1):
        along_x = ref[base + o : base + o + 8, :] + ref[base - o : base - o + 8, :]
        along_y = pltpu.roll(center, o, 1) + pltpu.roll(center, cols - o, 1)
        summed = summed + stencil_coef[o] * (along_x + along_y)
    return summed


def kernel(
    n, S, tile_rows,
    u_in, v_in, p_in, rate_in, mod, tmap, step0,
    out_u, out_v, out_g,
    Ub, Vb, Pb, Q, Fo, U1, Cb, W1, B1, W0, Fn, ends, Rown, Rpar, Am, Mp, E, RA, RE, X, G, Cx, Pre,
    part, gat1, gat2,
    load_sem, halo_s, halo_r, shift_s, shift_r, rate_s, rate_r, a_s, a_r, m_s, m_r, e_s, e_r,
    g_s, g_r, c_s, c_r, h_s, h_r, p_s, p_r, d1_s, d1_r, d2_s, d2_r,
):
    k = lax.axis_index("tm")
    s = lax.axis_index("strip")
    nc = n // 2
    c = k // 2
    j = k % 2
    partner = 2 * c + 1 - j
    R, C = out_u.shape
    H = R // 2
    W = H * C // (8 * nc)
    cpr = C // W

    def chip(d):
        return 2 * lax.rem(c + d + nc, nc) + j

    mine = pl.ds(pl.multiple_of(j * H, 8), H)
    other = pl.ds(pl.multiple_of((1 - j) * H, 8), H)
    loads = [
        pltpu.make_async_copy(u_in, Ub.at[pl.ds(BASE, R)], load_sem.at[0]),
        pltpu.make_async_copy(v_in, Vb.at[pl.ds(BASE, R)], load_sem.at[1]),
        pltpu.make_async_copy(p_in, Pb.at[pl.ds(BASE, R)], load_sem.at[2]),
        pltpu.make_async_copy(rate_in.at[mine], Rown, load_sem.at[3]),
    ]
    for load in loads:
        load.start()

    barrier = pltpu.get_barrier_semaphore()
    for d in range(1, nc):
        pl.semaphore_signal(barrier, inc=1, device_id=(chip(d), s), device_id_type=MESH)
    for d in range(1, 2 * S):
        at = lax.rem(s * 2 + j + d, 2 * S)
        pl.semaphore_signal(
            barrier, inc=1, device_id=(2 * c + at % 2, at // 2), device_id_type=MESH
        )
    aside = lax.rem(k + 2 * j - 1 + n, n)
    pl.semaphore_signal(barrier, inc=1, device_id=(aside, s), device_id_type=MESH)
    pl.semaphore_wait(barrier, (nc - 1) + (2 * S - 1) + 1)

    def remote(src, dst, ss, rs, where):
        return pltpu.make_async_remote_copy(
            src_ref=src, dst_ref=dst, send_sem=ss, recv_sem=rs,
            device_id=where, device_id_type=MESH,
        )

    up = lax.rem(s + S - 1, S)
    down = lax.rem(s + 1, S)
    tops = pl.ds(BASE - RIM, RIM)
    bottoms = pl.ds(BASE + R, RIM)
    has_up = s > 0
    has_down = s < S - 1
    fields = ((u_in, Ub), (v_in, Vb), (p_in, Pb))
    up_halo = [
        remote(a.at[pl.ds(0, RIM)], b.at[bottoms], halo_s.at[0, i], halo_r.at[0, i], (k, up))
        for i, (a, b) in enumerate(fields)
    ]
    down_halo = [
        remote(a.at[pl.ds(R - RIM, RIM)], b.at[tops], halo_s.at[1, i], halo_r.at[1, i], (k, down))
        for i, (a, b) in enumerate(fields)
    ]

    @pl.when(has_up)
    def _():
        for copy in up_halo:
            copy.start()

    @pl.when(has_down)
    def _():
        for copy in down_halo:
            copy.start()

    rate_copy = remote(rate_in.at[other], Rpar, rate_s, rate_r, (partner, s))
    rate_copy.start()
    before = lax.rem(k + n - 1, n)
    after = lax.rem(k + 1, n)
    shifts = [
        remote(u_in, Fn.at[0], shift_s.at[0], shift_r.at[0], (before, s)),
        remote(v_in, Fn.at[1], shift_s.at[1], shift_r.at[1], (before, s)),
    ]
    for copy in shifts:
        copy.start()

    zero = jnp.zeros((RIM, C), jnp.float32)
    Ub[0:RIM, :] = zero
    Ub[BASE + R + RIM : BASE + R + 2 * RIM, :] = zero
    W1[0:RIM, :] = zero
    W1[BASE + R + RIM : BASE + R + 2 * RIM, :] = zero

    @pl.when(jnp.logical_not(has_up))
    def _():
        Ub[BASE - RIM : BASE, :] = zero
        Vb[BASE - RIM : BASE, :] = zero
        Pb[BASE - RIM : BASE, :] = zero + 1.0
        Cb[0, BASE - RIM : BASE, :] = zero
        Cb[1, BASE - RIM : BASE, :] = zero

    @pl.when(jnp.logical_not(has_down))
    def _():
        Ub[BASE + R : BASE + R + RIM, :] = zero
        Vb[BASE + R : BASE + R + RIM, :] = zero
        Pb[BASE + R : BASE + R + RIM, :] = zero + 1.0
        Cb[0, BASE + R : BASE + R + RIM, :] = zero
        Cb[1, BASE + R : BASE + R + RIM, :] = zero

    loads[3].wait()
    rate_copy.wait_recv()
    for b in range(0, H, 8):
        own = jnp.exp(-Rown[b : b + 8, :] / n)
        par = jnp.exp(-Rpar[b : b + 8, :] / n)
        Rown[b : b + 8, :] = own
        Rpar[b : b + 8, :] = par
        Am[b : b + 8, :] = own * par

    def chunk(idx):
        return (
            pl.ds(pl.multiple_of((idx // cpr) * 8, 8), 8),
            pl.ds(pl.multiple_of((idx % cpr) * W, 128), W),
        )

    a_copies = []
    for d in range(1, nc):
        to = lax.rem(c + d, nc)
        rows, cols = chunk(to)
        copy = remote(Am.at[rows, cols], RA.at[d], a_s.at[d], a_r.at[d], (2 * to + j, s))
        copy.start()
        a_copies.append(copy)

    first = step0[0]
    cosines = [
        jnp.cos(
            jnp.float32(2.0 * jnp.pi / PERIOD)
            * jnp.full((8, 128), first + level, jnp.int32).astype(jnp.float32)
        )
        for level in range(STEPS)
    ]

    def depth_of(row):
        row = jnp.clip(row // TILE, 0, tile_rows - 1)
        return [mod[tmap[row, t]] for t in range(C // TILE)]

    def factors(depths):
        return [
            jnp.concatenate([1.0 + depth * cosines[level] for depth in depths], axis=1)
            for level in range(STEPS)
        ]

    first_row = s * R
    main_f = factors(depth_of(first_row))
    for copy in loads[:3]:
        copy.wait()

    def coefficients(base, fs):
        for level in range(STEPS):
            Q[level, base : base + 8, :] = time_step / (Pb[base : base + 8, :] * fs[level])

    for base in range(BASE, BASE + R, 8):
        coefficients(base, main_f)

    def first_step(base, keep):
        forcing = laplacian(Ub, base) - damping_rate * Vb[base : base + 8, :]
        speed = Vb[base : base + 8, :] + Q[0, base : base + 8, :] * forcing
        place = Ub[base : base + 8, :] + time_step * speed
        if keep is not None:
            place = place * keep
        Fo[0, base : base + 8, :] = forcing
        B1[base : base + 8, :] = speed
        U1[base : base + 8, :] = place

    for base in range(BASE + 8, BASE + R - 8, 8):
        first_step(base, None)

    @pl.when(has_down)
    def _():
        for copy in up_halo:
            copy.wait_recv()

    @pl.when(has_up)
    def _():
        for copy in down_halo:
            copy.wait_recv()

    coefficients(BASE - RIM, factors(depth_of(first_row - 1)))
    coefficients(BASE + R, factors(depth_of(first_row + R)))
    keep_top = has_up.astype(jnp.float32)
    keep_bottom = has_down.astype(jnp.float32)
    first_step(BASE - RIM, keep_top)
    first_step(BASE, None)
    first_step(BASE + R - 8, None)
    first_step(BASE + R, keep_bottom)

    for copy in shifts:
        copy.wait_recv()
    for base in range(BASE, BASE + R, 8):
        r = base - BASE
        forcing = laplacian(U1, base) - damping_rate * B1[base : base + 8, :]
        speed = B1[base : base + 8, :] + Q[1, base : base + 8, :] * forcing
        place = U1[base : base + 8, :] + time_step * speed
        Fo[1, base : base + 8, :] = forcing
        ends[0, r : r + 8, :] = place - Fn[0, r : r + 8, :]
        ends[1, r : r + 8, :] = speed - Fn[1, r : r + 8, :]

    m_copy = remote(ends.at[:, other], Mp, m_s, m_r, (partner, s))
    m_copy.start()
    m_copy.wait_recv()

    def half_rows(b):
        return pl.ds(pl.multiple_of(j * H + b, 8), 8)

    @pl.when(j == 0)
    def _():
        for b in range(0, H, 8):
            for f in range(2):
                E[f, b : b + 8, :] = (
                    ends[f, half_rows(b), :] + Rown[b : b + 8, :] * Mp[f, b : b + 8, :]
                )

    @pl.when(j == 1)
    def _():
        for b in range(0, H, 8):
            for f in range(2):
                E[f, b : b + 8, :] = (
                    Mp[f, b : b + 8, :] + Rpar[b : b + 8, :] * ends[f, half_rows(b), :]
                )

    e_copies = []
    for d in range(1, nc):
        to = lax.rem(c + d, nc)
        rows, cols = chunk(to)
        copy = remote(E.at[:, rows, cols], RE.at[d], e_s.at[d], e_r.at[d], (2 * to + j, s))
        copy.start()
        e_copies.append(copy)

    rows, cols = chunk(c)
    for copy in a_copies:
        copy.wait_recv()
    for copy in e_copies:
        copy.wait_recv()
    a0 = Am[rows, cols]
    total = a0
    state = [RE[1, f] for f in range(2)]
    total = total * RA[1]
    for d in range(2, nc):
        total = total * RA[d]
        state = [RA[d] * state[f] + RE[d, f] for f in range(2)]
    below = 1.0 / (1.0 - total)
    state = [(a0 * state[f] + E[f, rows, cols]) * below for f in range(2)]
    g_copies = []
    for d in range(1, nc):
        for f in range(2):
            X[d, f] = state[f]
        to = lax.rem(c - d + nc, nc)
        copy = remote(X.at[d], G.at[:, rows, cols], g_s.at[d], g_r.at[d], (2 * to + j, s))
        copy.start()
        g_copies.append(copy)
        state = [RA[d] * state[f] + RE[d, f] for f in range(2)]
    for f in range(2):
        G[f, rows, cols] = state[f]
    for copy in g_copies:
        copy.wait_recv()

    def main_half(b):
        return pl.ds(pl.multiple_of(BASE + j * H + b, 8), 8)

    @pl.when(j == 0)
    def _():
        for b in range(0, H, 8):
            for f in range(2):
                late = Rpar[b : b + 8, :] * G[f, b : b + 8, :] + Mp[f, b : b + 8, :]
                early = Rown[b : b + 8, :] * late + ends[f, half_rows(b), :]
                Cb[f, main_half(b), :] = early
                Cx[f, b : b + 8, :] = late

    @pl.when(j == 1)
    def _():
        for b in range(0, H, 8):
            for f in range(2):
                late = Rown[b : b + 8, :] * G[f, b : b + 8, :] + ends[f, half_rows(b), :]
                early = Rpar[b : b + 8, :] * late + Mp[f, b : b + 8, :]
                Cb[f, main_half(b), :] = late
                Cx[f, b : b + 8, :] = early

    main_mine = pl.ds(pl.multiple_of(BASE + j * H, 8), H)
    edge_cx = pl.ds(pl.multiple_of(j * (H - RIM), 8), RIM)
    edge_cb = pl.ds(pl.multiple_of(BASE + j * (R - RIM), 8), RIM)
    far = pl.ds(pl.multiple_of((1 - j) * (R + RIM) + BASE - RIM, 8), RIM)
    nb = lax.rem(s + 2 * j - 1 + S, S)
    c_copy = remote(Cx, Cb.at[:, main_mine], c_s, c_r, (partner, s))
    h_own = remote(Cb.at[:, edge_cb], Cb.at[:, far], h_s.at[0], h_r.at[j], (k, nb))
    h_par = remote(Cx.at[:, edge_cx], Cb.at[:, far], h_s.at[1], h_r.at[j], (partner, nb))
    sends_halo = jnp.where(j == 0, has_up.astype(jnp.int32), has_down.astype(jnp.int32)) == 1

    @pl.when(sends_halo)
    def _():
        h_own.start()
        h_par.start()

    c_copy.start()
    c_copy.wait_recv()
    p_copy = remote(Cb.at[:, pl.ds(BASE, R)], Pre, p_s, p_r, (after, s))
    p_copy.start()

    acc = jnp.zeros((8, C), jnp.float32)
    cos_cols = [jnp.concatenate([cosine] * (C // TILE), axis=1) for cosine in cosines]

    def weigh(base):
        total_v = Cb[1, base : base + 8, :] + time_step * Cb[0, base : base + 8, :]
        q = Q[1, base : base + 8, :]
        W1[base : base + 8, :] = q * total_v
        B1[base : base + 8, :] = (1.0 - damping_rate * q) * total_v
        return total_v, q

    for base in range(BASE, BASE + R, 8):
        total_v, q = weigh(base)
        acc = acc + Pb[base : base + 8, :] * cos_cols[1] * total_v * Fo[1, base : base + 8, :] * (q * q)

    @pl.when(has_up)
    def _():
        remote(Cb.at[:, edge_cb], Cb.at[:, tops], h_s.at[0], h_r.at[1], (k, nb)).wait_recv()

    @pl.when(has_down)
    def _():
        remote(Cb.at[:, edge_cb], Cb.at[:, bottoms], h_s.at[0], h_r.at[0], (k, nb)).wait_recv()

    weigh(BASE - RIM)
    weigh(BASE + R)

    def second(base, keep):
        back_u = Cb[0, base : base + 8, :] + laplacian(W1, base)
        total_v = B1[base : base + 8, :] + time_step * back_u
        q = Q[0, base : base + 8, :]
        weighted = q * total_v
        if keep is not None:
            weighted = weighted * keep
        W0[base : base + 8, :] = weighted
        return back_u, total_v, q

    second(BASE - RIM, keep_top)
    second(BASE + R, keep_bottom)
    for base in range(BASE, BASE + R, 8):
        r = base - BASE
        back_u, total_v, q = second(base, None)
        U1[base : base + 8, :] = back_u
        B1[base : base + 8, :] = (1.0 - damping_rate * q) * total_v
        acc = acc + Pb[base : base + 8, :] * cos_cols[0] * total_v * Fo[0, base : base + 8, :] * (q * q)

    lane = lax.broadcasted_iota(jnp.int32, (8, 128), 1)
    tile_row = first_row // TILE
    share = jnp.zeros((8, 128), jnp.float32)
    for t in range(C // TILE):
        summed = jnp.sum(acc[:, t * TILE : (t + 1) * TILE], axis=1, keepdims=True)
        share = share + jnp.where(lane == tmap[tile_row, t], summed, 0.0)
    part[0] = share * (-1.0 / time_step)
    d1 = []
    for d in range(1, nc):
        copy = remote(part.at[0], gat1.at[d], d1_s.at[d], d1_r.at[d], (chip(d), s))
        copy.start()
        d1.append(copy)

    p_copy.wait_recv()
    for base in range(BASE, BASE + R, 8):
        r = base - BASE
        out_u[r : r + 8, :] = U1[base : base + 8, :] + laplacian(W0, base) - Pre[0, r : r + 8, :]
        out_v[r : r + 8, :] = B1[base : base + 8, :] - Pre[1, r : r + 8, :]

    for copy in d1:
        copy.wait_recv()
    share = part[0]
    for d in range(1, nc):
        share = share + gat1[d]
    part[1] = share
    d2 = []
    for d in range(1, 2 * S):
        at = lax.rem(s * 2 + j + d, 2 * S)
        copy = remote(part.at[1], gat2.at[d], d2_s.at[d], d2_r.at[d], (2 * c + at % 2, at // 2))
        copy.start()
        d2.append(copy)
    for copy in d2:
        copy.wait_recv()
    for d in range(1, 2 * S):
        share = share + gat2[d]
    out_g[...] = jnp.sum(share, axis=0, keepdims=True)

    @pl.when(has_up)
    def _():
        for copy in up_halo:
            copy.wait_send()

    @pl.when(has_down)
    def _():
        for copy in down_halo:
            copy.wait_send()

    @pl.when(sends_halo)
    def _():
        h_own.wait_send()
        h_par.wait_send()

    for copy in [rate_copy, *shifts, *a_copies, m_copy, *e_copies, *g_copies, c_copy, p_copy, *d1, *d2]:
        copy.wait_send()


def solution(mesh):
    n = mesh.shape["tm"]
    S = mesh.shape["strip"]
    nc = n // 2

    def shards(forward_u, forward_v, permittivity, coarse_rate, modulation, tile_map, start_step):
        R, C = permittivity.shape
        H = R // 2
        W = H * C // (8 * nc)
        assert TILE % R == 0 and W % 128 == 0 and C % W == 0
        f32 = jnp.float32
        ext = R + 2 * BASE
        vmem = lambda *shape: pltpu.VMEM(shape, f32)
        dma = lambda *shape: pltpu.SemaphoreType.DMA(shape)
        any_spec = pl.BlockSpec(memory_space=pl.ANY)
        smem = pl.BlockSpec(memory_space=pltpu.SMEM)
        whole = pl.BlockSpec(memory_space=pltpu.VMEM)
        out_u, out_v, out_g = pl.pallas_call(
            functools.partial(kernel, n, S, tile_map.shape[0]),
            out_shape=(
                jax.ShapeDtypeStruct((R, C), f32),
                jax.ShapeDtypeStruct((R, C), f32),
                jax.ShapeDtypeStruct((1, 128), f32),
            ),
            in_specs=[any_spec] * 4 + [smem] * 3,
            out_specs=(whole, whole, whole),
            scratch_shapes=[
                vmem(ext, C), vmem(ext, C), vmem(ext, C), vmem(2, ext, C), vmem(2, ext, C),
                vmem(ext, C), vmem(2, ext, C), vmem(ext, C), vmem(ext, C), vmem(ext, C),
                vmem(2, R, C), vmem(2, R, C), vmem(H, C), vmem(H, C), vmem(H, C),
                vmem(2, H, C), vmem(2, H, C), vmem(nc, 8, W), vmem(nc, 2, 8, W),
                vmem(nc, 2, 8, W), vmem(2, H, C), vmem(2, H, C), vmem(2, R, C),
                vmem(2, 8, 128), vmem(nc, 8, 128), vmem(2 * S, 8, 128),
                dma(4), dma(2, 3), dma(2, 3), dma(2), dma(2), dma(), dma(), dma(nc), dma(nc),
                dma(), dma(), dma(nc), dma(nc), dma(nc), dma(nc), dma(), dma(), dma(2), dma(2),
                dma(), dma(), dma(nc), dma(nc), dma(2 * S), dma(2 * S),
            ],
            compiler_params=pltpu.CompilerParams(
                collective_id=0, has_side_effects=True, vmem_limit_bytes=48 * 1024 * 1024
            ),
        )(forward_u[0], forward_v[0], permittivity, coarse_rate[0], modulation, tile_map, start_step)
        return out_u[None], out_v[None], out_g[0, : modulation.shape[0]]

    placed = (
        P("tm", "strip", None),
        P("tm", "strip", None),
        P("strip", None),
        P("tm", "strip", None),
        P(),
        P(),
        P("tm"),
    )
    return jax.shard_map(
        shards,
        mesh=mesh,
        in_specs=placed,
        out_specs=(P("tm", "strip", None), P("tm", "strip", None), P()),
        check_vma=False,
    )
```

time: 253 us -> 54.6 us (0.22)
  the two profiles are of different devices: /device:TPU:0 before, /device:TPU:7 now
where the time goes in v1:
time: 54.6 us; the launch traced here: 54.3 us
  Pallas kernels  46.6 us (85%)
  local copies, waits for them, and re-layouts  6.37 us (12%)
  between operations  1.31 us (2%)
    pallas_call x1, Pallas kernels, shards(): pl.pallas_call(functools.partial(kernel, n, S, tile_map.shape[0]), out_sh...  46.6 us
    unnamed x14, local copies, waits for them, and re-layouts  5.86 us

profile of v1, /device:TPU:7, one launch (start us, length us, event | category | flops | bytes accessed | tf_op | source)
XLA Modules:
  0.0 54.3 jit_solution(4721207938545660774)
XLA Ops:
  1.3 0.0 copy-start.4
  1.3 0.0 copy-start.5
  1.3 0.6 %copy-done.4 = f32[32]{0:T(128)S(1)} copy-done((f32[32]{0:T(128)S(1)}, f32[32]{0:T(128)}, u32[]{:S(2)}) %copy-start.4) | copy-done | bytes 152
  1.9 0.0 copy-done.5
  2.0 0.0 copy-start
  2.0 0.9 %copy-done = f32[1,64,1024]{2,1,0:T(8,128)S(1)} copy-done((f32[1,64,1024]{2,1,0:T(8,128)S(1)}, f32[1,64,1024]{2,1,0:T(8,128)}, u32[]{:S(2)}) %copy-start) | copy-done | bytes 262168
  2.9 0.0 copy-start.1
  2.9 0.9 %copy-done.1 = f32[1,64,1024]{2,1,0:T(8,128)S(1)} copy-done((f32[1,64,1024]{2,1,0:T(8,128)S(1)}, f32[1,64,1024]{2,1,0:T(8,128)}, u32[]{:S(2)}) %copy-start.1) | copy-done | bytes 262168
  3.9 0.0 copy-start.2
  3.9 0.9 %copy-done.2 = f32[64,1024]{1,0:T(8,128)S(1)} copy-done((f32[64,1024]{1,0:T(8,128)S(1)}, f32[64,1024]{1,0:T(8,128)}, u32[]{:S(2)}) %copy-start.2) | copy-done | bytes 262168
  4.8 0.0 copy-start.3
  4.8 0.9 %copy-done.3 = f32[1,64,1024]{2,1,0:T(8,128)S(1)} copy-done((f32[1,64,1024]{2,1,0:T(8,128)S(1)}, f32[1,64,1024]{2,1,0:T(8,128)}, u32[]{:S(2)}) %copy-start.3) | copy-done | bytes 262168
  5.8 46.6 %shard_map.94 = (f32[64,1024]{1,0:T(8,128)S(1)}, f32[64,1024]{1,0:T(8,128)S(1)}, f32[1,128]{1,0:T(1,128)S(1)}) custom-call(f32[64,1024]{1,0:T(8,128)S(1)} %bitcast.7, f32[64,1024]{1,0:T(8,128)S(1)} %bitcast.8, f32[64,1024]{1,0:T(8,128)S(1)} %copy-done.2, f32[64,1024]{1,0:T(8,128)S(1)} %bitcast.9, f32[32]{0:T(128)S(1)} %copy-done.4, s32[1,8]{1,0:T(1,128)S(1)} %copy-done.5, ...), custom_call_target="tpu_custom_call" | custom-call | tf_op jit(solution)/shard_map/pallas_call | solution.py:460
  52.4 0.5 slice_bitcast_fusion
  52.9 0.7 %copy.13 = f32[1,64,1024]{2,1,0:T(8,128)} copy(f32[1,64,1024]{2,1,0:T(8,128)S(1)} %bitcast.11) | data formatting | bytes 524288
  53.6 0.7 %copy.14 = f32[1,64,1024]{2,1,0:T(8,128)} copy(f32[1,64,1024]{2,1,0:T(8,128)S(1)} %bitcast.10) | data formatting | bytes 524288
Async XLA Ops:
  1.3 0.7 %copy-start.4 = (f32[32]{0:T(128)S(1)}, f32[32]{0:T(128)}, u32[]{:S(2)}) copy-start(f32[32]{0:T(128)} %mod.1) | copy-start | bytes 388
  1.3 0.7 %copy-start.5 = (s32[1,8]{1,0:T(1,128)S(1)}, s32[1,8]{1,0:T(1,128)}, u32[]{:S(2)}) copy-start(s32[1,8]{1,0:T(1,128)} %tmap.1) | copy-start | bytes 100
  2.0 0.9 %copy-start = (f32[1,64,1024]{2,1,0:T(8,128)S(1)}, f32[1,64,1024]{2,1,0:T(8,128)}, u32[]{:S(2)}) copy-start(f32[1,64,1024]{2,1,0:T(8,128)} %param.7) | copy-start | bytes 786436
  2.9 0.9 %copy-start.1 = (f32[1,64,1024]{2,1,0:T(8,128)S(1)}, f32[1,64,1024]{2,1,0:T(8,128)}, u32[]{:S(2)}) copy-start(f32[1,64,1024]{2,1,0:T(8,128)} %param.8) | copy-start | bytes 786436
  3.9 0.9 %copy-start.2 = (f32[64,1024]{1,0:T(8,128)S(1)}, f32[64,1024]{1,0:T(8,128)}, u32[]{:S(2)}) copy-start(f32[64,1024]{1,0:T(8,128)} %p_in.1) | copy-start | bytes 786436
  4.8 0.9 %copy-start.3 = (f32[1,64,1024]{2,1,0:T(8,128)S(1)}, f32[1,64,1024]{2,1,0:T(8,128)}, u32[]{:S(2)}) copy-start(f32[1,64,1024]{2,1,0:T(8,128)} %param.10) | copy-start | bytes 786436

commit v2 on v1

--- a/solution.py
+++ b/solution.py
@@ -34,10 +34,10 @@
 
 def kernel(
     n, S, tile_rows,
-    u_in, v_in, p_in, rate_in, mod, tmap, step0,
+    u_in, v_in, p_in, rate_in, mod_in, tmap_in, step_in,
     out_u, out_v, out_g,
-    Ub, Vb, Pb, Q, Fo, U1, Cb, W1, B1, W0, Fn, ends, Rown, Rpar, Am, Mp, E, RA, RE, X, G, Cx, Pre,
-    part, gat1, gat2,
+    Ub, Vb, Pb, Q, Fo, U1, Cb, W1, B1, W0, Fp, ends, R0, R1, Am, Mp, Ep, E, RA, RE, X, G, Cx, Pre,
+    part, gat1, gat2, mod, tmap, step0,
     load_sem, halo_s, halo_r, shift_s, shift_r, rate_s, rate_r, a_s, a_r, m_s, m_r, e_s, e_r,
     g_s, g_r, c_s, c_r, h_s, h_r, p_s, p_r, d1_s, d1_r, d2_s, d2_r,
 ):
@@ -61,10 +61,18 @@
         pltpu.make_async_copy(u_in, Ub.at[pl.ds(BASE, R)], load_sem.at[0]),
         pltpu.make_async_copy(v_in, Vb.at[pl.ds(BASE, R)], load_sem.at[1]),
         pltpu.make_async_copy(p_in, Pb.at[pl.ds(BASE, R)], load_sem.at[2]),
-        pltpu.make_async_copy(rate_in.at[mine], Rown, load_sem.at[3]),
+        pltpu.make_async_copy(mod_in, mod, load_sem.at[4]),
+        pltpu.make_async_copy(tmap_in, tmap, load_sem.at[5]),
+        pltpu.make_async_copy(step_in, step0, load_sem.at[6]),
     ]
     for load in loads:
         load.start()
+
+    own_rate = pltpu.make_async_copy(rate_in.at[pl.ds(0, H)], R0, load_sem.at[3])
+
+    @pl.when(j == 0)
+    def _():
+        own_rate.start()
 
     barrier = pltpu.get_barrier_semaphore()
     for d in range(1, nc):
@@ -110,13 +118,27 @@
         for copy in down_halo:
             copy.start()
 
-    rate_copy = remote(rate_in.at[other], Rpar, rate_s, rate_r, (partner, s))
-    rate_copy.start()
-    before = lax.rem(k + n - 1, n)
-    after = lax.rem(k + 1, n)
+    low = pl.ds(0, H)
+    high = pl.ds(H, H)
+    c_next = lax.rem(c + 1, nc)
+    rate_pair = remote(rate_in.at[high], R0, rate_s.at[0], rate_r.at[0], (partner, s))
+    rate_next = [
+        remote(rate_in.at[low], R1, rate_s.at[0], rate_r.at[1], (2 * c_next, s)),
+        remote(rate_in.at[high], R1, rate_s.at[1], rate_r.at[1], (2 * c_next + 1, s)),
+    ]
+
+    @pl.when(j == 0)
+    def _():
+        rate_pair.start()
+
+    @pl.when(j == 1)
+    def _():
+        for copy in rate_next:
+            copy.start()
+
     shifts = [
-        remote(u_in, Fn.at[0], shift_s.at[0], shift_r.at[0], (before, s)),
-        remote(v_in, Fn.at[1], shift_s.at[1], shift_r.at[1], (before, s)),
+        remote(u_in.at[other], Fp.at[0], shift_s.at[0], shift_r.at[0], (partner, s)),
+        remote(v_in.at[other], Fp.at[1], shift_s.at[1], shift_r.at[1], (partner, s)),
     ]
     for copy in shifts:
         copy.start()
@@ -143,29 +165,14 @@
         Cb[0, BASE + R : BASE + R + RIM, :] = zero
         Cb[1, BASE + R : BASE + R + RIM, :] = zero
 
-    loads[3].wait()
-    rate_copy.wait_recv()
-    for b in range(0, H, 8):
-        own = jnp.exp(-Rown[b : b + 8, :] / n)
-        par = jnp.exp(-Rpar[b : b + 8, :] / n)
-        Rown[b : b + 8, :] = own
-        Rpar[b : b + 8, :] = par
-        Am[b : b + 8, :] = own * par
-
     def chunk(idx):
         return (
             pl.ds(pl.multiple_of((idx // cpr) * 8, 8), 8),
             pl.ds(pl.multiple_of((idx % cpr) * W, 128), W),
         )
 
-    a_copies = []
-    for d in range(1, nc):
-        to = lax.rem(c + d, nc)
-        rows, cols = chunk(to)
-        copy = remote(Am.at[rows, cols], RA.at[d], a_s.at[d], a_r.at[d], (2 * to + j, s))
-        copy.start()
-        a_copies.append(copy)
-
+    for copy in loads[3:]:
+        copy.wait()
     first = step0[0]
     cosines = [
         jnp.cos(
@@ -210,6 +217,29 @@
     for base in range(BASE + 8, BASE + R - 8, 8):
         first_step(base, None)
 
+    @pl.when(j == 0)
+    def _():
+        own_rate.wait()
+
+    @pl.when(j == 1)
+    def _():
+        rate_pair.wait_recv()
+
+    rate_next[0].wait_recv()
+    for b in range(0, H, 8):
+        own = jnp.exp(-R0[b : b + 8, :] / n)
+        R0[b : b + 8, :] = own
+        entering = jnp.exp(-R1[b : b + 8, :] / n)
+        R1[b : b + 8, :] = entering
+        Am[b : b + 8, :] = own * entering
+    a_copies = []
+    for d in range(1, nc):
+        to = lax.rem(c + d, nc)
+        rows, cols = chunk(to)
+        copy = remote(Am.at[rows, cols], RA.at[d], a_s.at[d], a_r.at[d], (2 * to + j, s))
+        copy.start()
+        a_copies.append(copy)
+
     @pl.when(has_down)
     def _():
         for copy in up_halo:
@@ -229,39 +259,49 @@
     first_step(BASE + R - 8, None)
     first_step(BASE + R, keep_bottom)
 
-    for copy in shifts:
-        copy.wait_recv()
     for base in range(BASE, BASE + R, 8):
         r = base - BASE
         forcing = laplacian(U1, base) - damping_rate * B1[base : base + 8, :]
         speed = B1[base : base + 8, :] + Q[1, base : base + 8, :] * forcing
         place = U1[base : base + 8, :] + time_step * speed
         Fo[1, base : base + 8, :] = forcing
-        ends[0, r : r + 8, :] = place - Fn[0, r : r + 8, :]
-        ends[1, r : r + 8, :] = speed - Fn[1, r : r + 8, :]
+        ends[0, r : r + 8, :] = place
+        ends[1, r : r + 8, :] = speed
 
     m_copy = remote(ends.at[:, other], Mp, m_s, m_r, (partner, s))
     m_copy.start()
+    for copy in shifts:
+        copy.wait_recv()
     m_copy.wait_recv()
 
-    def half_rows(b):
-        return pl.ds(pl.multiple_of(j * H + b, 8), 8)
+    def main_half(b):
+        return pl.ds(pl.multiple_of(BASE + j * H + b, 8), 8)
+
+    starts = (Ub, Vb)
 
     @pl.when(j == 0)
     def _():
         for b in range(0, H, 8):
+            entering = R1[b : b + 8, :]
             for f in range(2):
-                E[f, b : b + 8, :] = (
-                    ends[f, half_rows(b), :] + Rown[b : b + 8, :] * Mp[f, b : b + 8, :]
+                term = (
+                    ends[f, b : b + 8, :] - Fp[f, b : b + 8, :] + R0[b : b + 8, :] * Mp[f, b : b + 8, :]
                 )
+                Ep[f, b : b + 8, :] = term
+                E[f, b : b + 8, :] = entering * term - starts[f][BASE + b : BASE + b + 8, :]
 
     @pl.when(j == 1)
     def _():
         for b in range(0, H, 8):
+            entering = R1[b : b + 8, :]
             for f in range(2):
-                E[f, b : b + 8, :] = (
-                    Mp[f, b : b + 8, :] + Rpar[b : b + 8, :] * ends[f, half_rows(b), :]
+                term = (
+                    Mp[f, b : b + 8, :]
+                    - starts[f][BASE + H + b : BASE + H + b + 8, :]
+                    + R0[b : b + 8, :] * ends[f, H + b : H + b + 8, :]
                 )
+                Ep[f, b : b + 8, :] = term
+                E[f, b : b + 8, :] = entering * term - Fp[f, b : b + 8, :]
 
     e_copies = []
     for d in range(1, nc):
@@ -299,26 +339,23 @@
     for copy in g_copies:
         copy.wait_recv()
 
-    def main_half(b):
-        return pl.ds(pl.multiple_of(BASE + j * H + b, 8), 8)
-
     @pl.when(j == 0)
     def _():
         for b in range(0, H, 8):
             for f in range(2):
-                late = Rpar[b : b + 8, :] * G[f, b : b + 8, :] + Mp[f, b : b + 8, :]
-                early = Rown[b : b + 8, :] * late + ends[f, half_rows(b), :]
-                Cb[f, main_half(b), :] = early
-                Cx[f, b : b + 8, :] = late
+                value = G[f, b : b + 8, :]
+                Cx[f, b : b + 8, :] = value + Mp[f, b : b + 8, :]
+                Cb[f, BASE + b : BASE + b + 8, :] = R0[b : b + 8, :] * value + Ep[f, b : b + 8, :]
 
     @pl.when(j == 1)
     def _():
         for b in range(0, H, 8):
             for f in range(2):
-                late = Rown[b : b + 8, :] * G[f, b : b + 8, :] + ends[f, half_rows(b), :]
-                early = Rpar[b : b + 8, :] * late + Mp[f, b : b + 8, :]
-                Cb[f, main_half(b), :] = late
+                value = G[f, b : b + 8, :]
+                early = R0[b : b + 8, :] * value + Ep[f, b : b + 8, :]
+                Cb[f, BASE + H + b : BASE + H + b + 8, :] = value + ends[f, H + b : H + b + 8, :]
                 Cx[f, b : b + 8, :] = early
+                Pre[f, H + b : H + b + 8, :] = early
 
     main_mine = pl.ds(pl.multiple_of(BASE + j * H, 8), H)
     edge_cx = pl.ds(pl.multiple_of(j * (H - RIM), 8), RIM)
@@ -336,9 +373,20 @@
         h_par.start()
 
     c_copy.start()
+    p_low = remote(Cx, Pre.at[:, low], p_s.at[0], p_r.at[0], (2 * c_next, s))
+    p_pair = remote(Cb.at[:, main_mine], Pre.at[:, low], p_s.at[1], p_r.at[0], (partner, s))
+    p_high = remote(Cb.at[:, main_mine], Pre.at[:, high], p_s.at[0], p_r.at[1], (2 * c_next, s))
+
+    @pl.when(j == 0)
+    def _():
+        p_low.start()
+        p_pair.start()
+
+    @pl.when(j == 1)
+    def _():
+        p_high.start()
+
     c_copy.wait_recv()
-    p_copy = remote(Cb.at[:, pl.ds(BASE, R)], Pre, p_s, p_r, (after, s))
-    p_copy.start()
 
     acc = jnp.zeros((8, C), jnp.float32)
     cos_cols = [jnp.concatenate([cosine] * (C // TILE), axis=1) for cosine in cosines]
@@ -353,17 +401,6 @@
     for base in range(BASE, BASE + R, 8):
         total_v, q = weigh(base)
         acc = acc + Pb[base : base + 8, :] * cos_cols[1] * total_v * Fo[1, base : base + 8, :] * (q * q)
-
-    @pl.when(has_up)
-    def _():
-        remote(Cb.at[:, edge_cb], Cb.at[:, tops], h_s.at[0], h_r.at[1], (k, nb)).wait_recv()
-
-    @pl.when(has_down)
-    def _():
-        remote(Cb.at[:, edge_cb], Cb.at[:, bottoms], h_s.at[0], h_r.at[0], (k, nb)).wait_recv()
-
-    weigh(BASE - RIM)
-    weigh(BASE + R)
 
     def second(base, keep):
         back_u = Cb[0, base : base + 8, :] + laplacian(W1, base)
@@ -375,14 +412,29 @@
         W0[base : base + 8, :] = weighted
         return back_u, total_v, q
 
-    second(BASE - RIM, keep_top)
-    second(BASE + R, keep_bottom)
-    for base in range(BASE, BASE + R, 8):
-        r = base - BASE
+    def inner(base):
         back_u, total_v, q = second(base, None)
         U1[base : base + 8, :] = back_u
         B1[base : base + 8, :] = (1.0 - damping_rate * q) * total_v
-        acc = acc + Pb[base : base + 8, :] * cos_cols[0] * total_v * Fo[0, base : base + 8, :] * (q * q)
+        return Pb[base : base + 8, :] * cos_cols[0] * total_v * Fo[0, base : base + 8, :] * (q * q)
+
+    for base in range(BASE + 8, BASE + R - 8, 8):
+        acc = acc + inner(base)
+
+    @pl.when(has_up)
+    def _():
+        remote(Cb.at[:, edge_cb], Cb.at[:, tops], h_s.at[0], h_r.at[1], (k, nb)).wait_recv()
+
+    @pl.when(has_down)
+    def _():
+        remote(Cb.at[:, edge_cb], Cb.at[:, bottoms], h_s.at[0], h_r.at[0], (k, nb)).wait_recv()
+
+    weigh(BASE - RIM)
+    weigh(BASE + R)
+    second(BASE - RIM, keep_top)
+    second(BASE + R, keep_bottom)
+    acc = acc + inner(BASE)
+    acc = acc + inner(BASE + R - 8)
 
     lane = lax.broadcasted_iota(jnp.int32, (8, 128), 1)
     tile_row = first_row // TILE
@@ -397,11 +449,8 @@
         copy.start()
         d1.append(copy)
 
-    p_copy.wait_recv()
     for base in range(BASE, BASE + R, 8):
-        r = base - BASE
-        out_u[r : r + 8, :] = U1[base : base + 8, :] + laplacian(W0, base) - Pre[0, r : r + 8, :]
-        out_v[r : r + 8, :] = B1[base : base + 8, :] - Pre[1, r : r + 8, :]
+        U1[base : base + 8, :] = U1[base : base + 8, :] + laplacian(W0, base)
 
     for copy in d1:
         copy.wait_recv()
@@ -415,6 +464,16 @@
         copy = remote(part.at[1], gat2.at[d], d2_s.at[d], d2_r.at[d], (2 * c + at % 2, at // 2))
         copy.start()
         d2.append(copy)
+    p_low.wait_recv()
+
+    @pl.when(j == 0)
+    def _():
+        p_high.wait_recv()
+
+    for base in range(BASE, BASE + R, 8):
+        r = base - BASE
+        out_u[r : r + 8, :] = U1[base : base + 8, :] - Pre[0, r : r + 8, :]
+        out_v[r : r + 8, :] = B1[base : base + 8, :] - Pre[1, r : r + 8, :]
     for copy in d2:
         copy.wait_recv()
     for d in range(1, 2 * S):
@@ -436,8 +495,28 @@
         h_own.wait_send()
         h_par.wait_send()
 
-    for copy in [rate_copy, *shifts, *a_copies, m_copy, *e_copies, *g_copies, c_copy, p_copy, *d1, *d2]:
+    @pl.when(j == 0)
+    def _():
+        rate_pair.wait_send()
+        p_low.wait_send()
+        p_pair.wait_send()
+
+    @pl.when(j == 1)
+    def _():
+        for copy in [*rate_next, p_high]:
+            copy.wait_send()
+
+    for copy in [*shifts, *a_copies, m_copy, *e_copies, *g_copies, c_copy, *d1, *d2]:
         copy.wait_send()
+
+
+def store_outputs(u, v, g, out_u, out_v, out_g, sems):
+    pairs = ((u, out_u), (v, out_v), (g, out_g))
+    copies = [pltpu.make_async_copy(a, b, sems.at[i]) for i, (a, b) in enumerate(pairs)]
+    for copy in copies:
+        copy.start()
+    for copy in copies:
+        copy.wait()
 
 
 def solution(mesh):
@@ -455,7 +534,7 @@
         vmem = lambda *shape: pltpu.VMEM(shape, f32)
         dma = lambda *shape: pltpu.SemaphoreType.DMA(shape)
         any_spec = pl.BlockSpec(memory_space=pl.ANY)
-        smem = pl.BlockSpec(memory_space=pltpu.SMEM)
+        hbm = pl.BlockSpec(memory_space=pltpu.HBM)
         whole = pl.BlockSpec(memory_space=pltpu.VMEM)
         out_u, out_v, out_g = pl.pallas_call(
             functools.partial(kernel, n, S, tile_map.shape[0]),
@@ -464,23 +543,36 @@
                 jax.ShapeDtypeStruct((R, C), f32),
                 jax.ShapeDtypeStruct((1, 128), f32),
             ),
-            in_specs=[any_spec] * 4 + [smem] * 3,
+            in_specs=[hbm] * 7,
             out_specs=(whole, whole, whole),
             scratch_shapes=[
                 vmem(ext, C), vmem(ext, C), vmem(ext, C), vmem(2, ext, C), vmem(2, ext, C),
                 vmem(ext, C), vmem(2, ext, C), vmem(ext, C), vmem(ext, C), vmem(ext, C),
-                vmem(2, R, C), vmem(2, R, C), vmem(H, C), vmem(H, C), vmem(H, C),
-                vmem(2, H, C), vmem(2, H, C), vmem(nc, 8, W), vmem(nc, 2, 8, W),
+                vmem(2, H, C), vmem(2, R, C), vmem(H, C), vmem(H, C), vmem(H, C),
+                vmem(2, H, C), vmem(2, H, C), vmem(2, H, C), vmem(nc, 8, W), vmem(nc, 2, 8, W),
                 vmem(nc, 2, 8, W), vmem(2, H, C), vmem(2, H, C), vmem(2, R, C),
                 vmem(2, 8, 128), vmem(nc, 8, 128), vmem(2 * S, 8, 128),
-                dma(4), dma(2, 3), dma(2, 3), dma(2), dma(2), dma(), dma(), dma(nc), dma(nc),
+                pltpu.SMEM(modulation.shape, f32), pltpu.SMEM(tile_map.shape, jnp.int32),
+                pltpu.SMEM(start_step.shape, jnp.int32),
+                dma(7), dma(2, 3), dma(2, 3), dma(2), dma(2), dma(2), dma(2), dma(nc), dma(nc),
                 dma(), dma(), dma(nc), dma(nc), dma(nc), dma(nc), dma(), dma(), dma(2), dma(2),
-                dma(), dma(), dma(nc), dma(nc), dma(2 * S), dma(2 * S),
+                dma(2), dma(2), dma(nc), dma(nc), dma(2 * S), dma(2 * S),
             ],
             compiler_params=pltpu.CompilerParams(
                 collective_id=0, has_side_effects=True, vmem_limit_bytes=48 * 1024 * 1024
             ),
         )(forward_u[0], forward_v[0], permittivity, coarse_rate[0], modulation, tile_map, start_step)
+        out_u, out_v, out_g = pl.pallas_call(
+            store_outputs,
+            out_shape=(
+                jax.ShapeDtypeStruct((R, C), f32),
+                jax.ShapeDtypeStruct((R, C), f32),
+                jax.ShapeDtypeStruct((1, 128), f32),
+            ),
+            in_specs=[any_spec] * 3,
+            out_specs=(any_spec,) * 3,
+            scratch_shapes=[dma(3)],
+        )(out_u, out_v, out_g)
         return out_u[None], out_v[None], out_g[0, : modulation.shape[0]]
 
     placed = (

time: 54.6 us -> 66.5 us (1.22)
  the two profiles are of different devices: /device:TPU:7 before, /device:TPU:0 now
where the time goes in v2:
time: 66.5 us; the launch traced here: 66.2 us
  Pallas kernels  57.4 us (86%)
  local copies, waits for them, and re-layouts  7.5 us (11%)
  between operations  1.33 us (2%)
    pallas_call x1, Pallas kernels, shards(): pl.pallas_call(functools.partial(kernel, n, S, tile_map.shape[0]), out_sh...  40.4 us
    pallas_call x1, Pallas kernels, shards(): pl.pallas_call(store_outputs, out_shape=(jax.ShapeDtypeStruct((R, C), f32...  17 us
    unnamed x20, local copies, waits for them, and re-layouts  6.99 us

profile of v2, /device:TPU:0, one launch (start us, length us, event | category | flops | bytes accessed | tf_op | source)
XLA Modules:
  0.0 66.2 jit_solution(14631296759362496535)
XLA Ops:
  1.3 0.0 copy-start.6
  1.3 0.0 copy-start.7
  1.3 0.6 copy-done.6
  1.9 0.0 copy-done.7
  2.0 0.0 copy-start
  2.0 0.9 %copy-done = f32[1,64,1024]{2,1,0:T(8,128)S(1)} copy-done((f32[1,64,1024]{2,1,0:T(8,128)S(1)}, f32[1,64,1024]{2,1,0:T(8,128)}, u32[]{:S(2)}) %copy-start) | copy-done | bytes 262168
  2.9 0.0 copy-start.1
  2.9 0.9 %copy-done.1 = f32[1,64,1024]{2,1,0:T(8,128)S(1)} copy-done((f32[1,64,1024]{2,1,0:T(8,128)S(1)}, f32[1,64,1024]{2,1,0:T(8,128)}, u32[]{:S(2)}) %copy-start.1) | copy-done | bytes 262168
  3.9 0.0 copy-start.2
  3.9 0.9 %copy-done.2 = f32[64,1024]{1,0:T(8,128)S(1)} copy-done((f32[64,1024]{1,0:T(8,128)S(1)}, f32[64,1024]{1,0:T(8,128)}, u32[]{:S(2)}) %copy-start.2) | copy-done | bytes 262168
  4.8 0.0 copy-start.3
  4.8 0.9 %copy-done.3 = f32[1,64,1024]{2,1,0:T(8,128)S(1)} copy-done((f32[1,64,1024]{2,1,0:T(8,128)S(1)}, f32[1,64,1024]{2,1,0:T(8,128)}, u32[]{:S(2)}) %copy-start.3) | copy-done | bytes 262168
  5.8 40.4 %shard_map.94 = (f32[64,1024]{1,0:T(8,128)S(1)}, f32[64,1024]{1,0:T(8,128)S(1)}, f32[1,128]{1,0:T(1,128)S(1)}) custom-call(f32[64,1024]{1,0:T(8,128)S(1)} %bitcast.7, f32[64,1024]{1,0:T(8,128)S(1)} %bitcast.8, f32[64,1024]{1,0:T(8,128)S(1)} %copy-done.2, f32[64,1024]{1,0:T(8,128)S(1)} %bitcast.9, f32[32]{0:T(128)S(1)} %copy-done.6, s32[1,8]{1,0:T(1,128)S(1)} %copy-done.7, ...), custom_call_target="tpu_custom_call" | custom-call | tf_op jit(solution)/shard_map/pallas_call | solution.py:539
  46.1 0.0 copy-start.4
  46.1 0.7 %copy-done.4 = f32[64,1024]{1,0:T(8,128)} copy-done((f32[64,1024]{1,0:T(8,128)}, f32[64,1024]{1,0:T(8,128)S(1)}, u32[]{:S(2)}) %copy-start.4) | copy-done | bytes 262168
  46.8 0.0 copy-start.5
  46.8 0.7 %copy-done.5 = f32[64,1024]{1,0:T(8,128)} copy-done((f32[64,1024]{1,0:T(8,128)}, f32[64,1024]{1,0:T(8,128)S(1)}, u32[]{:S(2)}) %copy-start.5) | copy-done | bytes 262168
  47.5 0.0 copy-start.8
  47.5 0.5 copy-done.8
  48.0 17.0 %shard_map.95 = (f32[64,1024]{1,0:T(8,128)}, f32[64,1024]{1,0:T(8,128)}, f32[1,128]{1,0:T(1,128)}) custom-call(f32[64,1024]{1,0:T(8,128)} %copy-done.4, f32[64,1024]{1,0:T(8,128)} %copy-done.5, f32[1,128]{1,0:T(1,128)} %copy-done.8), custom_call_target="tpu_custom_call" | custom-call | tf_op jit(solution)/shard_map/pallas_call | solution.py:565
  65.1 0.0 copy-start.9
  65.1 0.6 copy-done.9
  65.7 0.5 slice_bitcast_fusion
Async XLA Ops:
  1.3 0.7 copy-start.6
  1.3 0.7 copy-start.7
  2.0 0.9 %copy-start = (f32[1,64,1024]{2,1,0:T(8,128)S(1)}, f32[1,64,1024]{2,1,0:T(8,128)}, u32[]{:S(2)}) copy-start(f32[1,64,1024]{2,1,0:T(8,128)} %param.7) | copy-start | bytes 786436
  2.9 0.9 %copy-start.1 = (f32[1,64,1024]{2,1,0:T(8,128)S(1)}, f32[1,64,1024]{2,1,0:T(8,128)}, u32[]{:S(2)}) copy-start(f32[1,64,1024]{2,1,0:T(8,128)} %param.8) | copy-start | bytes 786436
  3.9 0.9 %copy-start.2 = (f32[64,1024]{1,0:T(8,128)S(1)}, f32[64,1024]{1,0:T(8,128)}, u32[]{:S(2)}) copy-start(f32[64,1024]{1,0:T(8,128)} %p_in.1) | copy-start | bytes 786436
  4.8 0.9 %copy-start.3 = (f32[1,64,1024]{2,1,0:T(8,128)S(1)}, f32[1,64,1024]{2,1,0:T(8,128)}, u32[]{:S(2)}) copy-start(f32[1,64,1024]{2,1,0:T(8,128)} %param.10) | copy-start | bytes 786436
  46.1 0.7 %copy-start.4 = (f32[64,1024]{1,0:T(8,128)}, f32[64,1024]{1,0:T(8,128)S(1)}, u32[]{:S(2)}) copy-start(f32[64,1024]{1,0:T(8,128)S(1)} %get-tuple-element.9.u) | copy-start | bytes 786436
  46.8 0.7 %copy-start.5 = (f32[64,1024]{1,0:T(8,128)}, f32[64,1024]{1,0:T(8,128)S(1)}, u32[]{:S(2)}) copy-start(f32[64,1024]{1,0:T(8,128)S(1)} %get-tuple-element.10.v) | copy-start | bytes 786436
  47.5 0.5 copy-start.8
  65.1 0.6 copy-start.9

commit v3 on v2

--- a/solution.py
+++ b/solution.py
@@ -510,13 +510,10 @@
         copy.wait_send()
 
 
-def store_outputs(u, v, g, out_u, out_v, out_g, sems):
-    pairs = ((u, out_u), (v, out_v), (g, out_g))
-    copies = [pltpu.make_async_copy(a, b, sems.at[i]) for i, (a, b) in enumerate(pairs)]
-    for copy in copies:
-        copy.start()
-    for copy in copies:
-        copy.wait()
+def store_outputs(u, v, g, out_u, out_v, out_g):
+    out_u[...] = u[...]
+    out_v[...] = v[...]
+    out_g[...] = g[...]
 
 
 def solution(mesh):
@@ -536,6 +533,9 @@
         any_spec = pl.BlockSpec(memory_space=pl.ANY)
         hbm = pl.BlockSpec(memory_space=pltpu.HBM)
         whole = pl.BlockSpec(memory_space=pltpu.VMEM)
+        operands = (
+            forward_u[0], forward_v[0], permittivity, coarse_rate[0], modulation, tile_map, start_step
+        )
         out_u, out_v, out_g = pl.pallas_call(
             functools.partial(kernel, n, S, tile_map.shape[0]),
             out_shape=(
@@ -561,7 +561,7 @@
             compiler_params=pltpu.CompilerParams(
                 collective_id=0, has_side_effects=True, vmem_limit_bytes=48 * 1024 * 1024
             ),
-        )(forward_u[0], forward_v[0], permittivity, coarse_rate[0], modulation, tile_map, start_step)
+        )(*[pltpu.with_memory_space_constraint(a, pltpu.HBM) for a in operands[:6]], operands[6])
         out_u, out_v, out_g = pl.pallas_call(
             store_outputs,
             out_shape=(
@@ -569,9 +569,9 @@
                 jax.ShapeDtypeStruct((R, C), f32),
                 jax.ShapeDtypeStruct((1, 128), f32),
             ),
-            in_specs=[any_spec] * 3,
-            out_specs=(any_spec,) * 3,
-            scratch_shapes=[dma(3)],
+            in_specs=[whole] * 3,
+            out_specs=(whole,) * 3,
+            compiler_params=pltpu.CompilerParams(vmem_limit_bytes=8*1024*1024),
         )(out_u, out_v, out_g)
         return out_u[None], out_v[None], out_g[0, : modulation.shape[0]]
 

time: 66.5 us -> 42.5 us (0.64)
  Pallas kernels: 57.4 us -> 40.5 us
  local copies, waits for them, and re-layouts: 7.5 us -> 0.51 us
    pallas_call x1, Pallas kernels: 17 us -> 0.82 us  [shards(): pl.pallas_call(store_outputs, out_shape=(jax.ShapeDtypeStruct((R, C), f32...]
    unnamed x20 -> x0, local copies, waits for them, and re-layouts: 6.99 us -> none
    pallas_call x1, Pallas kernels: 40.4 us -> 39.7 us  [shards(): pl.pallas_call(functools.partial(kernel, n, S, tile_map.shape[0]), out_sh...]
where the time goes in v3:
time: 42.5 us; the launch traced here: 42.3 us
  Pallas kernels  40.5 us (95%)
  between operations  1.29 us (3%)
  local copies, waits for them, and re-layouts  0.51 us (1%)
    pallas_call x1, Pallas kernels, shards(): pl.pallas_call(functools.partial(kernel, n, S, tile_map.shape[0]), out_sh...  39.7 us

profile of v3, /device:TPU:0, one launch (start us, length us, event | category | flops | bytes accessed | tf_op | source)
XLA Modules:
  0.0 42.3 jit_solution(7129008126504498811)
XLA Ops:
  1.3 39.7 %shard_map.94 = (f32[64,1024]{1,0:T(8,128)S(1)}, f32[64,1024]{1,0:T(8,128)S(1)}, f32[1,128]{1,0:T(1,128)S(1)}) custom-call(f32[64,1024]{1,0:T(8,128)} %bitcast.7, f32[64,1024]{1,0:T(8,128)} %bitcast.8, f32[64,1024]{1,0:T(8,128)} %p_in.1, f32[64,1024]{1,0:T(8,128)} %bitcast.9, f32[32]{0:T(128)} %mod_in.1, s32[1,8]{1,0:T(1,128)} %tmap_in.1, s32[1]{0:T(128)S(6)} %copy.10.step_in), custom_call_target="tpu_custom_call" | custom-call | tf_op jit(solution)/shard_map/pallas_call | solution.py:539
  40.9 0.8 %shard_map.95 = (f32[64,1024]{1,0:T(8,128)}, f32[64,1024]{1,0:T(8,128)}, f32[1,128]{1,0:T(1,128)S(1)}) custom-call(f32[64,1024]{1,0:T(8,128)S(1)} %get-tuple-element.9.u, f32[64,1024]{1,0:T(8,128)S(1)} %get-tuple-element.10.v, f32[1,128]{1,0:T(1,128)S(1)} %get-tuple-element.11.g), custom_call_target="tpu_custom_call" | custom-call | tf_op jit(solution)/shard_map/pallas_call | solution.py:565
  41.8 0.5 %slice_bitcast_fusion = f32[32]{0:T(128)} fusion(f32[1,128]{1,0:T(1,128)S(1)} %get-tuple-element.14), kind=kLoop, calls=%fused_computation | loop fusion | bytes 256 | tf_op jit(solution)/shard_map/squeeze | solution.py:576

commit v4 on v3

--- a/solution.py
+++ b/solution.py
@@ -52,6 +52,8 @@
     W = H * C // (8 * nc)
     cpr = C // W
 
+    turns = sorted(range(1, nc), key=lambda d: (-min(d, nc - d), d))
+
     def chip(d):
         return 2 * lax.rem(c + d + nc, nc) + j
 
@@ -233,7 +235,7 @@
         R1[b : b + 8, :] = entering
         Am[b : b + 8, :] = own * entering
     a_copies = []
-    for d in range(1, nc):
+    for d in turns:
         to = lax.rem(c + d, nc)
         rows, cols = chunk(to)
         copy = remote(Am.at[rows, cols], RA.at[d], a_s.at[d], a_r.at[d], (2 * to + j, s))
@@ -304,7 +306,7 @@
                 E[f, b : b + 8, :] = entering * term - Fp[f, b : b + 8, :]
 
     e_copies = []
-    for d in range(1, nc):
+    for d in turns:
         to = lax.rem(c + d, nc)
         rows, cols = chunk(to)
         copy = remote(E.at[:, rows, cols], RE.at[d], e_s.at[d], e_r.at[d], (2 * to + j, s))
@@ -513,7 +515,7 @@
 def store_outputs(u, v, g, out_u, out_v, out_g):
     out_u[...] = u[...]
     out_v[...] = v[...]
-    out_g[...] = g[...]
+    out_g[...] = g[0, : out_g.shape[0]]
 
 
 def solution(mesh):
@@ -567,13 +569,13 @@
             out_shape=(
                 jax.ShapeDtypeStruct((R, C), f32),
                 jax.ShapeDtypeStruct((R, C), f32),
-                jax.ShapeDtypeStruct((1, 128), f32),
+                jax.ShapeDtypeStruct(modulation.shape, f32),
             ),
             in_specs=[whole] * 3,
             out_specs=(whole,) * 3,
             compiler_params=pltpu.CompilerParams(vmem_limit_bytes=8*1024*1024),
         )(out_u, out_v, out_g)
-        return out_u[None], out_v[None], out_g[0, : modulation.shape[0]]
+        return out_u[None], out_v[None], out_g
 
     placed = (
         P("tm", "strip", None),

time: 42.5 us -> 41.6 us (0.979)
  local copies, waits for them, and re-layouts: 0.51 us -> 0 us
    squeeze x1 -> x0, local copies, waits for them, and re-layouts: 0.51 us -> none  [shards(): return (out_u[None], out_v[None], out_g[0, :modulation.shape[0]])]
where the time goes in v4:
time: 41.6 us; the launch traced here: 41.4 us
  Pallas kernels  40.1 us (96%)
  between operations  1.29 us (3%)
    pallas_call x1, Pallas kernels, shards(): pl.pallas_call(functools.partial(kernel, n, S, tile_map.shape[0]), out_sh...  39.3 us

profile of v4, /device:TPU:0, one launch (start us, length us, event | category | flops | bytes accessed | tf_op | source)
XLA Modules:
  0.0 41.4 jit_solution(2374507622532541714)
XLA Ops:
  1.3 39.3 %shard_map.94 = (f32[64,1024]{1,0:T(8,128)S(1)}, f32[64,1024]{1,0:T(8,128)S(1)}, f32[1,128]{1,0:T(1,128)S(1)}) custom-call(f32[64,1024]{1,0:T(8,128)} %bitcast.5, f32[64,1024]{1,0:T(8,128)} %bitcast.6, f32[64,1024]{1,0:T(8,128)} %p_in.1, f32[64,1024]{1,0:T(8,128)} %bitcast.7, f32[32]{0:T(128)} %mod_in.1, s32[1,8]{1,0:T(1,128)} %tmap_in.1, s32[1]{0:T(128)S(6)} %copy.10.step_in), custom_call_target="tpu_custom_call" | custom-call | tf_op jit(solution)/shard_map/pallas_call | solution.py:541
  40.6 0.8 %shard_map.95 = (f32[64,1024]{1,0:T(8,128)}, f32[64,1024]{1,0:T(8,128)}, f32[32]{0:T(128)}) custom-call(f32[64,1024]{1,0:T(8,128)S(1)} %get-tuple-element.9.u, f32[64,1024]{1,0:T(8,128)S(1)} %get-tuple-element.10.v, f32[1,128]{1,0:T(1,128)S(1)} %get-tuple-element.11.g), custom_call_target="tpu_custom_call" | custom-call | tf_op jit(solution)/shard_map/pallas_call | solution.py:567
